TPU v7x, 256 devices: a whole 4x4x8 slice. The times are simulated.
256 devices in a mesh: tm: 32 (over z, x), fsdp: 8 (over y, core).
Axes of the slice: x: 4, y: 4, z: 8, core: 2. Of those that a mesh axis runs over, the one named last changes fastest.
Arguments:
- frames: bfloat16 [64, 64, 256, 128], P('tm', None, 'fsdp'), may hold values from -6 to 6
- conv_weight: bfloat16 [3, 3, 3, 128, 128], P(None, None, None, None, 'fsdp'), may hold values from -0.109375 to 0.109375
- mix_weight: bfloat16 [3, 128, 128], P(None, None, 'fsdp'), may hold values from -0.3125 to 0.3125
- cotangent: bfloat16 [32, 64, 256, 128], P(None, 'tm', 'fsdp'), may hold values from -0.008239746 to 0.008239746
Outputs:
- encoded: bfloat16 [32, 64, 256, 128], P(None, 'tm', 'fsdp')
- mix_grad: float32 [49152], P(('tm', 'fsdp'))
All inputs are finite; a program needn't handle non-finite values.
Results may differ from a plain program's by a relative error of at most 0.0058.
Values may be sent and summed in bfloat16 or wider, within the bound.
A program may use at most 64 MiB of HBM per device.

v0:
```python
import jax
import jax.numpy as jnp
from jax import lax
from jax.sharding import PartitionSpec as P


def from_behind(block, axis, distance):
    devices = range(lax.axis_size(axis))
    route = [(i - distance, i) for i in devices if i - distance in devices]
    return lax.ppermute(block, axis, route)


def with_halo(cells, sides, width):
    for axis, dim in sides:
        count = lax.axis_size(axis)
        ends = count - 1
        head = lax.slice_in_dim(cells, 0, width, axis=dim)
        tail = lax.slice_in_dim(cells, cells.shape[dim] - width, cells.shape[dim], axis=dim)
        cells = jnp.concatenate(
            [
                lax.ppermute(tail, axis, [(i, (i + 1) % count) for i in range(ends)]),
                cells,
                lax.ppermute(head, axis, [((i + 1) % count, i) for i in range(ends)]),
            ],
            axis=dim,
        )
    return cells


def pool_pairs(hidden):
    shaped = hidden.reshape((hidden.shape[0] // 2, 2) + hidden.shape[1:]).astype(jnp.float32)
    return ((shaped[:, 0] + shaped[:, 1]) * 0.5).astype(jnp.bfloat16)


def delayed(block, offset):
    return jnp.pad(block, ((offset, 0), (0, 0), (0, 0), (0, 0)))[: block.shape[0]]


def local(frames, conv_weight, mix_weight, cotangent):
    full_conv, full_mix = (
        lax.all_gather(conv_weight, "fsdp", axis=4, tiled=True),
        lax.all_gather(mix_weight, "fsdp", axis=2, tiled=True),
    )
    count_frames, height, width, channels = frames.shape
    previous = from_behind(frames, "tm", 1)
    timed = jnp.concatenate([previous, frames], axis=0)
    padded = with_halo(timed, (("fsdp", 2),), 1)
    padded = jnp.pad(padded, ((0, 0), (1, 1), (0, 0), (0, 0)))
    accum = jnp.zeros((count_frames * height * width, channels), jnp.float32)
    for row_tap in range(3):
        for col_tap in range(3):
            stacked = jnp.concatenate(
                [
                    padded[
                        step : step + count_frames,
                        row_tap : row_tap + height,
                        col_tap : col_tap + width,
                        :,
                    ]
                    for step in range(3)
                ],
                axis=3,
            ).reshape(-1, 3 * channels)
            kernel = full_conv[:, row_tap, col_tap].reshape(3 * channels, channels)
            accum = accum + jnp.dot(stacked, kernel, preferred_element_type=jnp.float32)
    hidden = jax.nn.silu(accum).astype(jnp.bfloat16).reshape(count_frames, height, width, channels)
    pooled = lax.all_to_all(pool_pairs(hidden), "tm", split_axis=1, concat_axis=0, tiled=True)
    branch = pooled.astype(jnp.float32).reshape(-1, channels)
    flat_cot = cotangent.reshape(-1, channels)
    grad_terms = []
    for offset in range(3):
        lagged = delayed(pooled, offset).reshape(-1, channels)
        branch = branch + jnp.dot(lagged, full_mix[offset], preferred_element_type=jnp.float32)
        grad_terms.append(
            lax.dot_general(
                lagged, flat_cot, (((0,), (0,)), ((), ())), preferred_element_type=jnp.float32
            )
        )
    encoded = branch.astype(jnp.bfloat16).reshape(pooled.shape)
    parts = lax.axis_size("tm") * lax.axis_size("fsdp")
    mix_grad = lax.all_to_all(
        jnp.stack(grad_terms).reshape(parts, -1), ("tm", "fsdp"), 0, 0, tiled=True
    ).sum(0)
    return (encoded, mix_grad)


def solution(mesh):
    return jax.shard_map(
        local,
        mesh=mesh,
        in_specs=(
            P("tm", None, "fsdp", None),
            P(None, None, None, None, "fsdp"),
            P(None, None, "fsdp"),
            P(None, "tm", "fsdp", None),
        ),
        out_specs=(P(None, "tm", "fsdp", None), P(("tm", "fsdp"))),
        check_vma=False,
    )
```

profile of v0, /device:TPU:1, one launch (start us, length us, event | category | flops | bytes accessed | tf_op | source)
XLA Modules:
  0.0 129.5 jit_solution(5271844698895392121)
XLA Ops:
  0.7 4.1 %collective-permute-start = (bf16[2,64,32,128]{3,2,1,0:T(8,128)(2,1)}, bf16[2,64,32,128]{3,2,1,0:T(8,128)(2,1)S(1)}, u32[]{:S(2)}, u32[]{:S(2)}) collective-permute-start(bf16[2,64,32,128]{3,2,1,0:T(8,128)(2,1)} %param.4), channel_id=1, source_target_pairs={{0,8},{8,16},{16,24},{24,32},{32,40},{40,48},{48,56},{56,64},{64,7... | collective-permute-start | bytes 3145736 | tf_op jit(solution)/shard_map/ppermute | solution.py:10
  4.8 15.0 %all_gather.6 = bf16[3,3,3,128,128]{3,4,2,1,0:T(8,128)(2,1)S(1)} all-gather(bf16[3,3,3,128,16]{3,4,2,1,0:T(8,128)(2,1)} %param.5), channel_id=1, replica_groups=mesh['tm'=32,'fsdp'=8] {'fsdp'}, dimensions={4}, use_global_device_ids=true | all-gather | bytes 995328 | tf_op jit(solution)/shard_map/all_gather | solution.py:41
  19.8 7.0 %collective-permute-done = bf16[2,64,32,128]{3,2,1,0:T(8,128)(2,1)S(1)} collective-permute-done((bf16[2,64,32,128]{3,2,1,0:T(8,128)(2,1)}, bf16[2,64,32,128]{3,2,1,0:T(8,128)(2,1)S(1)}, u32[]{:S(2)}, u32[]{:S(2)}) %collective-permute-start) | collective-permute-done | bytes 1048608 | tf_op jit(solution)/shard_map/ppermute | solution.py:10
  28.0 3.4 %collective-permute-start.2 = (bf16[4,64,1,128]{3,2,1,0:T(2,128)(2,1)}, bf16[4,64,1,128]{3,2,1,0:T(2,128)(2,1)S(1)}, u32[]{:S(2)}, u32[]{:S(2)}) collective-permute-start(bf16[4,64,1,128]{3,2,1,0:T(2,128)(2,1)} %get-tuple-element.30), channel_id=1, source_target_pairs={{1,0},{2,1},{3,2},{4,3},{5,4},{6,5},{7,6},{9,8},{10,9},{11,10},{12... | collective-permute-start | bytes 196616 | tf_op jit(solution)/shard_map/ppermute | solution.py:23
  31.5 3.1 %collective-permute-start.1 = (bf16[4,64,1,128]{3,2,1,0:T(2,128)(2,1)}, bf16[4,64,1,128]{3,2,1,0:T(2,128)(2,1)S(1)}, u32[]{:S(2)}, u32[]{:S(2)}) collective-permute-start(bf16[4,64,1,128]{3,2,1,0:T(2,128)(2,1)} %get-tuple-element.29), channel_id=1, source_target_pairs={{0,1},{1,2},{2,3},{3,4},{4,5},{5,6},{6,7},{8,9},{9,10},{10,11},{11... | collective-permute-start | bytes 196616 | tf_op jit(solution)/shard_map/ppermute | solution.py:21
  35.3 1.6 %copy.19 = bf16[3,1,1,128,128]{4,3,0,2,1:T(8,128)(2,1)} copy(bf16[3,1,1,128,128]{3,4,2,1,0:T(8,128)(2,1)} %get-tuple-element.39) | data formatting | bytes 196608
  39.4 1.6 %copy.27 = bf16[3,1,1,128,128]{4,3,0,2,1:T(8,128)(2,1)} copy(bf16[3,1,1,128,128]{3,4,2,1,0:T(8,128)(2,1)} %get-tuple-element.31) | data formatting | bytes 196608
  41.1 1.5 %fusion.7 = bf16[4,66,34,128]{3,2,1,0:T(8,128)(2,1)S(1)} fusion(bf16[4,64,1,128]{3,2,1,0:T(2,128)(2,1)S(1)} %collective-permute-done.2, bf16[4,64,32,128]{3,2,1,0:T(8,128)(2,1)S(1)} %constant_dynamic-update-slice_fusion, bf16[4,64,1,128]{3,2,1,0:T(2,128)(2,1)S(1)} %collective-permute-done.1), kind=kLoop, calls=%fused_computation.30 | loop fusion | flops 13787136 | bytes 4526080 | tf_op jit(solution)/shard_map/concatenate | solution.py:19
  42.6 6.9 %fusion.16 = (bf16[2,64,32,128]{3,2,1,0:T(8,128)(2,1)S(1)}, bf16[2,64,32,128]{3,2,1,0:T(8,128)(2,1)S(1)}, bf16[2,64,32,128]{3,2,1,0:T(8,128)(2,1)S(1)}, bf16[2,6...) fusion(bf16[4,66,34,128]{3,2,1,0:T(8,128)(2,1)S(1)} %fusion.7), kind=kLoop, calls=%fused_computation.59 | loop fusion | bytes 37748736 | tf_op jit(solution)/shard_map/slice | solution.py:54
  49.5 3.3 %pad_maximum_fusion.2 = (bf16[2,64,32,384]{3,2,1,0:T(8,128)(2,1)S(1)}, bf16[2,64,32,384]{3,2,1,0:T(8,128)(2,1)S(1)}) fusion(bf16[2,64,32,128]{3,2,1,0:T(8,128)(2,1)} %get-tuple-element.16, bf16[2,64,32,128]{3,2,1,0:T(8,128)(2,1)} %get-tuple-element.17, bf16[2,64,32,128]{3,2,1,0:T(8,128)(2,1)} %get-tuple-element.18, ...), kind=kLoop, calls=%fused_computation.19 | loop fusion | flops 18874368 | bytes 12582912 | tf_op jit(solution)/shard_map/concatenate | solution.py:52
  53.9 1.1 convolution_add_fusion.7
  57.8 2.1 %fusion.10 = (bf16[2,64,32,128]{3,2,1,0:T(8,128)(2,1)S(1)}, bf16[2,64,32,128]{3,2,1,0:T(8,128)(2,1)S(1)}, bf16[2,64,32,128]{3,2,1,0:T(8,128)(2,1)S(1)}, bf16[2,6...) fusion(bf16[4,64,32,128]{3,2,1,0:T(8,128)(2,1)S(1)} %constant_dynamic-update-slice_fusion, ...), kind=kLoop, calls=%fused_computation.44 | loop fusion | flops 8388608 | bytes 8650752 | tf_op jit(solution)/shard_map/concatenate | solution.py:19
  60.0 2.5 %fusion.1 = (bf16[2,64,32,384]{3,2,1,0:T(8,128)(2,1)S(1)}, bf16[2,64,32,384]{3,2,1,0:T(8,128)(2,1)S(1)}) fusion(bf16[4,64,1,128]{3,2,1,0:T(2,128)(2,1)S(1)} %collective-permute-done.2, bf16[4,64,32,128]{3,2,1,0:T(8,128)(2,1)S(1)} %constant_dynamic-update-slice_fusion, bf16[2,64,32,128]{3,2,1,0:T(8,128)(2,1)S(1)} %get-tuple-element.21, ...), kind=kLoop, calls=%fused_computation.16 | loop fusion | flops 25165824 | bytes 12713984 | tf_op jit(solution)/shard_map/concatenate | solution.py:52
  66.5 1.0 convolution_add_fusion.2
  68.4 1.0 convolution_add_fusion.1
  69.5 1.1 multiply_convert_fusion
  70.9 1.0 fusion.15
  71.9 12.8 %all-to-all-start = ((bf16[1,64,32,128]{3,2,0,1:T(8,128)(2,1)}), bf16[1,64,32,128]{3,2,0,1:T(8,128)(2,1)S(1)}, u32[]{:S(2)}, u32[]{:S(2)}) async-start(bf16[1,64,32,128]{3,2,0,1:T(8,128)(2,1)} %fusion.15), calls=%async_computation | async-start | bytes 1048576 | tf_op jit(solution)/shard_map/all_to_all | solution.py:67
  84.8 12.7 %all_gather.7 = bf16[3,128,128]{1,2,0:T(8,128)(2,1)S(1)} all-gather(bf16[3,128,16]{1,2,0:T(8,128)(2,1)S(1)} %copy-done.12), channel_id=1, replica_groups=mesh['tm'=32,'fsdp'=8] {'fsdp'}, dimensions={2}, use_global_device_ids=true | all-gather | bytes 110592 | tf_op jit(solution)/shard_map/all_gather | solution.py:42
  97.4 4.7 %all-to-all-done = bf16[1,64,32,128]{3,2,0,1:T(8,128)(2,1)S(1)} async-done(((bf16[1,64,32,128]{3,2,0,1:T(8,128)(2,1)}), bf16[1,64,32,128]{3,2,0,1:T(8,128)(2,1)S(1)}, u32[]{:S(2)}, u32[]{:S(2)}) %all-to-all-start) | async-done | bytes 524320 | tf_op jit(solution)/shard_map/all_to_all | solution.py:67
  103.7 1.1 all_to_all.22
  104.9 8.5 %all-to-all-start.1 = ((f32[256,1,192]{2,1,0:T(1,128)}), f32[256,1,192]{2,1,0:T(1,128)S(1)}, u32[]{:S(2)}, u32[]{:S(2)}) async-start(f32[256,1,192]{2,1,0:T(1,128)} %all_to_all.22), calls=%async_computation.1 | async-start | bytes 524288 | tf_op jit(solution)/shard_map/all_to_all | solution.py:81
  113.7 1.1 fusion.8
  114.8 13.9 %all-to-all-done.1 = f32[256,1,192]{2,1,0:T(1,128)S(1)} async-done(((f32[256,1,192]{2,1,0:T(1,128)}), f32[256,1,192]{2,1,0:T(1,128)S(1)}, u32[]{:S(2)}, u32[]{:S(2)}) %all-to-all-start.1) | async-done | bytes 196640 | tf_op jit(solution)/shard_map/all_to_all | solution.py:81
  (56 shorter events, 16.0 us)
Async XLA Ops:
  0.6 101.7 %copy-start = (bf16[32,2,32,128]{3,2,1,0:T(8,128)(2,1)S(1)}, bf16[32,2,32,128]{3,2,1,0:T(8,128)(2,1)}, u32[]{:S(2)}) copy-start(bf16[32,2,32,128]{3,2,1,0:T(8,128)(2,1)} %param.7) | copy-start | bytes 1572868
  0.6 26.3 %copy-start.5 = (bf16[2,64,32,128]{3,2,1,0:T(8,128)(2,1)S(1)}, bf16[2,64,32,128]{3,2,1,0:T(8,128)(2,1)}, u32[]{:S(2)}) copy-start(bf16[2,64,32,128]{3,2,1,0:T(8,128)(2,1)} %param.4) | copy-start | bytes 3145732
  0.7 26.2 %collective-permute-start = (bf16[2,64,32,128]{3,2,1,0:T(8,128)(2,1)}, bf16[2,64,32,128]{3,2,1,0:T(8,128)(2,1)S(1)}, u32[]{:S(2)}, u32[]{:S(2)}) collective-permute-start(bf16[2,64,32,128]{3,2,1,0:T(8,128)(2,1)} %param.4), channel_id=1, source_target_pairs={{0,8},{8,16},{16,24},{24,32},{32,40},{40,48},{48,56},{56,64},{64,7... | collective-permute-start | bytes 3145736 | tf_op jit(solution)/shard_map/ppermute | solution.py:10
  26.9 8.5 %copy-start.7 = (bf16[2,64,32,128]{3,2,1,0:T(8,128)(2,1)}, bf16[2,64,32,128]{3,2,1,0:T(8,128)(2,1)S(1)}, u32[]{:S(2)}) copy-start(bf16[2,64,32,128]{3,2,1,0:T(8,128)(2,1)S(1)} %collective-permute-done) | copy-start | bytes 3145732
  28.0 13.0 %collective-permute-start.2 = (bf16[4,64,1,128]{3,2,1,0:T(2,128)(2,1)}, bf16[4,64,1,128]{3,2,1,0:T(2,128)(2,1)S(1)}, u32[]{:S(2)}, u32[]{:S(2)}) collective-permute-start(bf16[4,64,1,128]{3,2,1,0:T(2,128)(2,1)} %get-tuple-element.30), channel_id=1, source_target_pairs={{1,0},{2,1},{3,2},{4,3},{5,4},{6,5},{7,6},{9,8},{10,9},{11,10},{12... | collective-permute-start | bytes 196616 | tf_op jit(solution)/shard_map/ppermute | solution.py:23
  31.5 9.6 %collective-permute-start.1 = (bf16[4,64,1,128]{3,2,1,0:T(2,128)(2,1)}, bf16[4,64,1,128]{3,2,1,0:T(2,128)(2,1)S(1)}, u32[]{:S(2)}, u32[]{:S(2)}) collective-permute-start(bf16[4,64,1,128]{3,2,1,0:T(2,128)(2,1)} %get-tuple-element.29), channel_id=1, source_target_pairs={{0,1},{1,2},{2,3},{3,4},{4,5},{5,6},{6,7},{8,9},{9,10},{10,11},{11... | collective-permute-start | bytes 196616 | tf_op jit(solution)/shard_map/ppermute | solution.py:21
  49.5 3.3 %copy-start.10 = (bf16[3,1,1,128,128]{4,3,0,2,1:T(8,128)(2,1)S(1)}, bf16[3,1,1,128,128]{4,3,0,2,1:T(8,128)(2,1)}, u32[]{:S(2)}) copy-start(bf16[3,1,1,128,128]{4,3,0,2,1:T(8,128)(2,1)} %copy.19) | copy-start | bytes 294916
  52.8 1.0 copy-start.9
  53.8 1.2 copy-start.1
  53.8 1.5 %copy-start.2 = (bf16[2,64,32,128]{3,2,1,0:T(8,128)(2,1)S(1)}, bf16[2,64,32,128]{3,2,1,0:T(8,128)(2,1)}, u32[]{:S(2)}) copy-start(bf16[2,64,32,128]{3,2,1,0:T(8,128)(2,1)} %get-tuple-element.10) | copy-start | bytes 3145732
  53.8 1.8 %copy-start.3 = (bf16[2,64,32,128]{3,2,1,0:T(8,128)(2,1)S(1)}, bf16[2,64,32,128]{3,2,1,0:T(8,128)(2,1)}, u32[]{:S(2)}) copy-start(bf16[2,64,32,128]{3,2,1,0:T(8,128)(2,1)} %get-tuple-element.11) | copy-start | bytes 3145732
  53.8 2.1 %copy-start.4 = (bf16[2,64,32,128]{3,2,1,0:T(8,128)(2,1)S(1)}, bf16[2,64,32,128]{3,2,1,0:T(8,128)(2,1)}, u32[]{:S(2)}) copy-start(bf16[2,64,32,128]{3,2,1,0:T(8,128)(2,1)} %get-tuple-element.12) | copy-start | bytes 3145732
  62.5 1.2 copy-start.6
  62.5 1.5 %copy-start.8 = (bf16[2,64,32,128]{3,2,1,0:T(8,128)(2,1)S(1)}, bf16[2,64,32,128]{3,2,1,0:T(8,128)(2,1)}, u32[]{:S(2)}) copy-start(bf16[2,64,32,128]{3,2,1,0:T(8,128)(2,1)} %copy-done.7) | copy-start | bytes 3145732
  68.4 1.0 copy-start.11
  70.6 14.1 %copy-start.12 = (bf16[3,128,16]{1,2,0:T(8,128)(2,1)S(1)}, bf16[3,128,16]{1,2,0:T(8,128)(2,1)}, u32[]{:S(2)}) copy-start(bf16[3,128,16]{1,2,0:T(8,128)(2,1)} %param.6) | copy-start | bytes 36868
  71.9 30.2 %all-to-all-start = ((bf16[1,64,32,128]{3,2,0,1:T(8,128)(2,1)}), bf16[1,64,32,128]{3,2,0,1:T(8,128)(2,1)S(1)}, u32[]{:S(2)}, u32[]{:S(2)}) async-start(bf16[1,64,32,128]{3,2,0,1:T(8,128)(2,1)} %fusion.15), calls=%async_computation | async-start | bytes 1048576 | tf_op jit(solution)/shard_map/all_to_all | solution.py:67
  104.9 23.8 %all-to-all-start.1 = ((f32[256,1,192]{2,1,0:T(1,128)}), f32[256,1,192]{2,1,0:T(1,128)S(1)}, u32[]{:S(2)}, u32[]{:S(2)}) async-start(f32[256,1,192]{2,1,0:T(1,128)} %all_to_all.22), calls=%async_computation.1 | async-start | bytes 524288 | tf_op jit(solution)/shard_map/all_to_all | solution.py:81
where the time goes:
time: 130 us
  starting transfers between devices  32 us (25%)
  blocking collectives  27.7 us (21%)
  waiting for transfers between devices  25.6 us (20%)
  local copies, waits for them, and re-layouts  17.5 us (13%)
  other arithmetic  13.8 us (11%)
  matrix products  11.9 us (9%)
    all_gather x1, blocking collectives, local(): lax.all_gather(conv_weight, 'fsdp', axis=4, tiled=True)  15 us
    all_to_all x1, waiting for transfers between devices, local(): lax.all_to_all(jnp.stack(grad_terms).reshape(parts, -1), ('tm', 'fsdp'),...  13.9 us
    all_to_all x1, starting transfers between devices, local(): lax.all_to_all(pool_pairs(hidden), 'tm', split_axis=1, concat_axis=0, til...  12.8 us
    all_gather x1, blocking collectives, local(): lax.all_gather(mix_weight, 'fsdp', axis=2, tiled=True)  12.7 us
    dot_general x9, matrix products, local(): accum = accum + jnp.dot(stacked, kernel, preferred_element_type=jnp.float32)  9.18 us
    all_to_all x1, starting transfers between devices, local(): lax.all_to_all(jnp.stack(grad_terms).reshape(parts, -1), ('tm', 'fsdp'),...  8.54 us
    concatenate x5, other arithmetic, local(): jnp.concatenate([padded[step:step + count_frames, row_tap:row_tap + heigh...  7.93 us
    unnamed x36, local copies, waits for them, and re-layouts  7.4 us
  transfers between devices with their start and end apart: 5, of which 3 were waited for; matrix products, arithmetic and copies ran while one was open for 6% of the time, Pallas kernels for 0%

commit v1 on v0

--- a/solution.py
+++ b/solution.py
@@ -38,7 +38,9 @@
 
 def local(frames, conv_weight, mix_weight, cotangent):
     full_conv, full_mix = (
-        lax.all_gather(conv_weight, "fsdp", axis=4, tiled=True),
+        jnp.concatenate(
+            lax.all_to_all(jnp.stack([conv_weight] * lax.psum(1, "fsdp")), "fsdp", 0, 0), axis=4
+        ),
         lax.all_gather(mix_weight, "fsdp", axis=2, tiled=True),
     )
     count_frames, height, width, channels = frames.shape

time: 130 us -> 130 us (level)
  waiting for transfers between devices: 25.6 us -> 20.6 us
  blocking collectives: 27.7 us -> 31.4 us
  local copies, waits for them, and re-layouts: 17.5 us -> 18.8 us
    all_to_all x0 -> x1, blocking collectives: none -> 18.7 us  [local(): lax.all_to_all(jnp.stack([conv_weight] * lax.psum(1, 'fsdp')), 'fsdp', 0, 0)]
    all_gather x1 -> x0, blocking collectives: 15 us -> none  [local(): lax.all_gather(conv_weight, 'fsdp', axis=4, tiled=True)]
    slice x1 -> x10, local copies, waits for them, and re-layouts: 0.76 us -> 6.43 us  [local(): kernel = full_conv[:, row_tap, col_tap].reshape(3 * channels, channels)]
    unnamed x36 -> x27, local copies, waits for them, and re-layouts: 7.4 us -> 1.73 us
    ppermute x1, waiting for transfers between devices: 7.05 us -> 2.09 us  [from_behind(): return lax.ppermute(block, axis, route)]
  transfers between devices with their start and end apart: 5 -> 5, of which waited for: 3 -> 3; matrix products, arithmetic and copies ran while one was open for 6% -> 7% of each run, Pallas kernels for 0% -> 0%
where the time goes in v1:
time: 130 us
  starting transfers between devices  32 us (25%)
  blocking collectives  31.4 us (24%)
  waiting for transfers between devices  20.6 us (16%)
  local copies, waits for them, and re-layouts  18.8 us (14%)
  other arithmetic  13.8 us (11%)
  matrix products  11.9 us (9%)
    all_to_all x1, blocking collectives, local(): lax.all_to_all(jnp.stack([conv_weight] * lax.psum(1, 'fsdp')), 'fsdp', 0, 0)  18.7 us
    all_to_all x1, waiting for transfers between devices, local(): lax.all_to_all(jnp.stack(grad_terms).reshape(parts, -1), ('tm', 'fsdp'),...  13.9 us
    all_to_all x1, starting transfers between devices, local(): lax.all_to_all(pool_pairs(hidden), 'tm', split_axis=1, concat_axis=0, til...  12.8 us
    all_gather x1, blocking collectives, local(): lax.all_gather(mix_weight, 'fsdp', axis=2, tiled=True)  12.7 us
    dot_general x9, matrix products, local(): accum = accum + jnp.dot(stacked, kernel, preferred_element_type=jnp.float32)  9.18 us
    all_to_all x1, starting transfers between devices, local(): lax.all_to_all(jnp.stack(grad_terms).reshape(parts, -1), ('tm', 'fsdp'),...  8.54 us
    concatenate x5, other arithmetic, local(): jnp.concatenate([padded[step:step + count_frames, row_tap:row_tap + heigh...  7.93 us
    slice x1, local copies, waits for them, and re-layouts, local(): padded[step:step + count_frames, row_tap:row_tap + height, col_tap:col_ta...  6.92 us
  transfers between devices with their start and end apart: 5, of which 3 were waited for; matrix products, arithmetic and copies ran while one was open for 7% of the time, Pallas kernels for 0%

profile of v1, /device:TPU:1, one launch (start us, length us, event | category | flops | bytes accessed | tf_op | source)
XLA Modules:
  0.0 129.5 jit_solution(9501929181668379913)
XLA Ops:
  0.7 4.1 %collective-permute-start = (bf16[2,64,32,128]{3,2,1,0:T(8,128)(2,1)}, bf16[2,64,32,128]{3,2,1,0:T(8,128)(2,1)S(1)}, u32[]{:S(2)}, u32[]{:S(2)}) collective-permute-start(bf16[2,64,32,128]{3,2,1,0:T(8,128)(2,1)} %param.4), channel_id=1, source_target_pairs={{0,8},{8,16},{16,24},{24,32},{32,40},{40,48},{48,56},{56,64},{64,7... | collective-permute-start | bytes 3145736 | tf_op jit(solution)/shard_map/ppermute | solution.py:10
  5.8 18.7 %all_to_all.30 = bf16[8,3,3,3,128,16]{4,5,3,2,1,0:T(8,128)(2,1)S(1)} all-to-all(bf16[8,3,3,3,128,16]{4,5,3,2,1,0:T(8,128)(2,1)S(1)} %stack.10), channel_id=1, replica_groups=mesh['tm'=32,'fsdp'=8] {'fsdp'}, dimensions={0} | all-to-all | bytes 1769472 | tf_op jit(solution)/shard_map/all_to_all | solution.py:42
  24.8 2.1 %collective-permute-done = bf16[2,64,32,128]{3,2,1,0:T(8,128)(2,1)S(1)} collective-permute-done((bf16[2,64,32,128]{3,2,1,0:T(8,128)(2,1)}, bf16[2,64,32,128]{3,2,1,0:T(8,128)(2,1)S(1)}, u32[]{:S(2)}, u32[]{:S(2)}) %collective-permute-start) | collective-permute-done | bytes 1048608 | tf_op jit(solution)/shard_map/ppermute | solution.py:10
  28.0 3.4 %collective-permute-start.2 = (bf16[4,64,1,128]{3,2,1,0:T(2,128)(2,1)}, bf16[4,64,1,128]{3,2,1,0:T(2,128)(2,1)S(1)}, u32[]{:S(2)}, u32[]{:S(2)}) collective-permute-start(bf16[4,64,1,128]{3,2,1,0:T(2,128)(2,1)} %get-tuple-element.30), channel_id=1, source_target_pairs={{1,0},{2,1},{3,2},{4,3},{5,4},{6,5},{7,6},{9,8},{10,9},{11,10},{12... | collective-permute-start | bytes 196616 | tf_op jit(solution)/shard_map/ppermute | solution.py:23
  31.5 3.1 %collective-permute-start.1 = (bf16[4,64,1,128]{3,2,1,0:T(2,128)(2,1)}, bf16[4,64,1,128]{3,2,1,0:T(2,128)(2,1)S(1)}, u32[]{:S(2)}, u32[]{:S(2)}) collective-permute-start(bf16[4,64,1,128]{3,2,1,0:T(2,128)(2,1)} %get-tuple-element.29), channel_id=1, source_target_pairs={{0,1},{1,2},{2,3},{3,4},{4,5},{5,6},{6,7},{8,9},{9,10},{10,11},{11... | collective-permute-start | bytes 196616 | tf_op jit(solution)/shard_map/ppermute | solution.py:21
  35.3 1.6 %copy.17 = bf16[3,1,1,128,128]{4,3,0,2,1:T(8,128)(2,1)} copy(bf16[3,1,1,128,128]{3,4,2,1,0:T(8,128)(2,1)} %get-tuple-element.39) | data formatting | bytes 196608 | tf_op jit(solution)/shard_map/slice | solution.py:66
  39.4 1.6 %copy.25 = bf16[3,1,1,128,128]{4,3,0,2,1:T(8,128)(2,1)} copy(bf16[3,1,1,128,128]{3,4,2,1,0:T(8,128)(2,1)} %get-tuple-element.31) | data formatting | bytes 196608 | tf_op jit(solution)/shard_map/slice | solution.py:66
  41.1 1.5 %fusion.7 = bf16[4,66,34,128]{3,2,1,0:T(8,128)(2,1)S(1)} fusion(bf16[4,64,1,128]{3,2,1,0:T(2,128)(2,1)S(1)} %collective-permute-done.2, bf16[4,64,32,128]{3,2,1,0:T(8,128)(2,1)S(1)} %constant_dynamic-update-slice_fusion, bf16[4,64,1,128]{3,2,1,0:T(2,128)(2,1)S(1)} %collective-permute-done.1), kind=kLoop, calls=%fused_computation.30 | loop fusion | flops 13787136 | bytes 4526080 | tf_op jit(solution)/shard_map/concatenate | solution.py:19
  42.6 6.9 %fusion.16 = (bf16[2,64,32,128]{3,2,1,0:T(8,128)(2,1)S(1)}, bf16[2,64,32,128]{3,2,1,0:T(8,128)(2,1)S(1)}, bf16[2,64,32,128]{3,2,1,0:T(8,128)(2,1)S(1)}, bf16[2,6...) fusion(bf16[4,66,34,128]{3,2,1,0:T(8,128)(2,1)S(1)} %fusion.7), kind=kLoop, calls=%fused_computation.59 | loop fusion | bytes 37748736 | tf_op jit(solution)/shard_map/slice | solution.py:56
  49.5 3.3 %pad_maximum_fusion.2 = (bf16[2,64,32,384]{3,2,1,0:T(8,128)(2,1)S(1)}, bf16[2,64,32,384]{3,2,1,0:T(8,128)(2,1)S(1)}) fusion(bf16[2,64,32,128]{3,2,1,0:T(8,128)(2,1)} %get-tuple-element.16, bf16[2,64,32,128]{3,2,1,0:T(8,128)(2,1)} %get-tuple-element.17, bf16[2,64,32,128]{3,2,1,0:T(8,128)(2,1)} %get-tuple-element.18, ...), kind=kLoop, calls=%fused_computation.19 | loop fusion | flops 18874368 | bytes 12582912 | tf_op jit(solution)/shard_map/concatenate | solution.py:54
  53.9 1.1 convolution_add_fusion.7
  57.8 2.1 %fusion.10 = (bf16[2,64,32,128]{3,2,1,0:T(8,128)(2,1)S(1)}, bf16[2,64,32,128]{3,2,1,0:T(8,128)(2,1)S(1)}, bf16[2,64,32,128]{3,2,1,0:T(8,128)(2,1)S(1)}, bf16[2,6...) fusion(bf16[4,64,32,128]{3,2,1,0:T(8,128)(2,1)S(1)} %constant_dynamic-update-slice_fusion, ...), kind=kLoop, calls=%fused_computation.44 | loop fusion | flops 8388608 | bytes 8650752 | tf_op jit(solution)/shard_map/concatenate | solution.py:19
  60.0 2.5 %fusion.1 = (bf16[2,64,32,384]{3,2,1,0:T(8,128)(2,1)S(1)}, bf16[2,64,32,384]{3,2,1,0:T(8,128)(2,1)S(1)}) fusion(bf16[4,64,1,128]{3,2,1,0:T(2,128)(2,1)S(1)} %collective-permute-done.2, bf16[4,64,32,128]{3,2,1,0:T(8,128)(2,1)S(1)} %constant_dynamic-update-slice_fusion, bf16[2,64,32,128]{3,2,1,0:T(8,128)(2,1)S(1)} %get-tuple-element.21, ...), kind=kLoop, calls=%fused_computation.16 | loop fusion | flops 25165824 | bytes 12713984 | tf_op jit(solution)/shard_map/concatenate | solution.py:54
  66.5 1.0 convolution_add_fusion.2
  68.4 1.0 convolution_add_fusion.1
  69.5 1.1 multiply_convert_fusion
  70.9 1.0 fusion.15
  71.9 12.8 %all-to-all-start.1 = ((bf16[1,64,32,128]{3,2,0,1:T(8,128)(2,1)}), bf16[1,64,32,128]{3,2,0,1:T(8,128)(2,1)S(1)}, u32[]{:S(2)}, u32[]{:S(2)}) async-start(bf16[1,64,32,128]{3,2,0,1:T(8,128)(2,1)} %fusion.15), calls=%async_computation.1 | async-start | bytes 1048576 | tf_op jit(solution)/shard_map/all_to_all | solution.py:69
  84.8 12.7 %all_gather.3 = bf16[3,128,128]{1,2,0:T(8,128)(2,1)S(1)} all-gather(bf16[3,128,16]{1,2,0:T(8,128)(2,1)S(1)} %copy-done.12), channel_id=1, replica_groups=mesh['tm'=32,'fsdp'=8] {'fsdp'}, dimensions={2}, use_global_device_ids=true | all-gather | bytes 110592 | tf_op jit(solution)/shard_map/all_gather | solution.py:44
  97.4 4.7 %all-to-all-done.1 = bf16[1,64,32,128]{3,2,0,1:T(8,128)(2,1)S(1)} async-done(((bf16[1,64,32,128]{3,2,0,1:T(8,128)(2,1)}), bf16[1,64,32,128]{3,2,0,1:T(8,128)(2,1)S(1)}, u32[]{:S(2)}, u32[]{:S(2)}) %all-to-all-start.1) | async-done | bytes 524320 | tf_op jit(solution)/shard_map/all_to_all | solution.py:69
  103.7 1.1 all_to_all.26
  104.9 8.5 %all-to-all-start.2 = ((f32[256,1,192]{2,1,0:T(1,128)}), f32[256,1,192]{2,1,0:T(1,128)S(1)}, u32[]{:S(2)}, u32[]{:S(2)}) async-start(f32[256,1,192]{2,1,0:T(1,128)} %all_to_all.26), calls=%async_computation.2 | async-start | bytes 524288 | tf_op jit(solution)/shard_map/all_to_all | solution.py:83
  113.7 1.1 fusion.8
  114.8 13.9 %all-to-all-done.2 = f32[256,1,192]{2,1,0:T(1,128)S(1)} async-done(((f32[256,1,192]{2,1,0:T(1,128)}), f32[256,1,192]{2,1,0:T(1,128)S(1)}, u32[]{:S(2)}, u32[]{:S(2)}) %all-to-all-start.2) | async-done | bytes 196640 | tf_op jit(solution)/shard_map/all_to_all | solution.py:83
  (58 shorter events, 17.3 us)
Async XLA Ops:
  0.6 101.7 %copy-start = (bf16[32,2,32,128]{3,2,1,0:T(8,128)(2,1)S(1)}, bf16[32,2,32,128]{3,2,1,0:T(8,128)(2,1)}, u32[]{:S(2)}) copy-start(bf16[32,2,32,128]{3,2,1,0:T(8,128)(2,1)} %param.7) | copy-start | bytes 1572868
  0.6 26.3 %copy-start.5 = (bf16[2,64,32,128]{3,2,1,0:T(8,128)(2,1)S(1)}, bf16[2,64,32,128]{3,2,1,0:T(8,128)(2,1)}, u32[]{:S(2)}) copy-start(bf16[2,64,32,128]{3,2,1,0:T(8,128)(2,1)} %param.4) | copy-start | bytes 3145732
  0.7 26.2 %collective-permute-start = (bf16[2,64,32,128]{3,2,1,0:T(8,128)(2,1)}, bf16[2,64,32,128]{3,2,1,0:T(8,128)(2,1)S(1)}, u32[]{:S(2)}, u32[]{:S(2)}) collective-permute-start(bf16[2,64,32,128]{3,2,1,0:T(8,128)(2,1)} %param.4), channel_id=1, source_target_pairs={{0,8},{8,16},{16,24},{24,32},{32,40},{40,48},{48,56},{56,64},{64,7... | collective-permute-start | bytes 3145736 | tf_op jit(solution)/shard_map/ppermute | solution.py:10
  26.9 8.5 %copy-start.7 = (bf16[2,64,32,128]{3,2,1,0:T(8,128)(2,1)}, bf16[2,64,32,128]{3,2,1,0:T(8,128)(2,1)S(1)}, u32[]{:S(2)}) copy-start(bf16[2,64,32,128]{3,2,1,0:T(8,128)(2,1)S(1)} %collective-permute-done) | copy-start | bytes 3145732
  28.0 13.0 %collective-permute-start.2 = (bf16[4,64,1,128]{3,2,1,0:T(2,128)(2,1)}, bf16[4,64,1,128]{3,2,1,0:T(2,128)(2,1)S(1)}, u32[]{:S(2)}, u32[]{:S(2)}) collective-permute-start(bf16[4,64,1,128]{3,2,1,0:T(2,128)(2,1)} %get-tuple-element.30), channel_id=1, source_target_pairs={{1,0},{2,1},{3,2},{4,3},{5,4},{6,5},{7,6},{9,8},{10,9},{11,10},{12... | collective-permute-start | bytes 196616 | tf_op jit(solution)/shard_map/ppermute | solution.py:23
  31.5 9.6 %collective-permute-start.1 = (bf16[4,64,1,128]{3,2,1,0:T(2,128)(2,1)}, bf16[4,64,1,128]{3,2,1,0:T(2,128)(2,1)S(1)}, u32[]{:S(2)}, u32[]{:S(2)}) collective-permute-start(bf16[4,64,1,128]{3,2,1,0:T(2,128)(2,1)} %get-tuple-element.29), channel_id=1, source_target_pairs={{0,1},{1,2},{2,3},{3,4},{4,5},{5,6},{6,7},{8,9},{9,10},{10,11},{11... | collective-permute-start | bytes 196616 | tf_op jit(solution)/shard_map/ppermute | solution.py:21
  49.5 3.3 %copy-start.10 = (bf16[3,1,1,128,128]{4,3,0,2,1:T(8,128)(2,1)S(1)}, bf16[3,1,1,128,128]{4,3,0,2,1:T(8,128)(2,1)}, u32[]{:S(2)}) copy-start(bf16[3,1,1,128,128]{4,3,0,2,1:T(8,128)(2,1)} %copy.17) | copy-start | bytes 294916
  52.8 1.0 copy-start.9
  53.8 1.2 copy-start.1
  53.8 1.5 %copy-start.2 = (bf16[2,64,32,128]{3,2,1,0:T(8,128)(2,1)S(1)}, bf16[2,64,32,128]{3,2,1,0:T(8,128)(2,1)}, u32[]{:S(2)}) copy-start(bf16[2,64,32,128]{3,2,1,0:T(8,128)(2,1)} %get-tuple-element.10) | copy-start | bytes 3145732
  53.8 1.8 %copy-start.3 = (bf16[2,64,32,128]{3,2,1,0:T(8,128)(2,1)S(1)}, bf16[2,64,32,128]{3,2,1,0:T(8,128)(2,1)}, u32[]{:S(2)}) copy-start(bf16[2,64,32,128]{3,2,1,0:T(8,128)(2,1)} %get-tuple-element.11) | copy-start | bytes 3145732
  53.8 2.1 %copy-start.4 = (bf16[2,64,32,128]{3,2,1,0:T(8,128)(2,1)S(1)}, bf16[2,64,32,128]{3,2,1,0:T(8,128)(2,1)}, u32[]{:S(2)}) copy-start(bf16[2,64,32,128]{3,2,1,0:T(8,128)(2,1)} %get-tuple-element.12) | copy-start | bytes 3145732
  62.5 1.2 copy-start.6
  62.5 1.5 %copy-start.8 = (bf16[2,64,32,128]{3,2,1,0:T(8,128)(2,1)S(1)}, bf16[2,64,32,128]{3,2,1,0:T(8,128)(2,1)}, u32[]{:S(2)}) copy-start(bf16[2,64,32,128]{3,2,1,0:T(8,128)(2,1)} %copy-done.7) | copy-start | bytes 3145732
  68.4 1.0 copy-start.11
  70.6 14.1 %copy-start.12 = (bf16[3,128,16]{1,2,0:T(8,128)(2,1)S(1)}, bf16[3,128,16]{1,2,0:T(8,128)(2,1)}, u32[]{:S(2)}) copy-start(bf16[3,128,16]{1,2,0:T(8,128)(2,1)} %param.6) | copy-start | bytes 36868
  71.9 30.2 %all-to-all-start.1 = ((bf16[1,64,32,128]{3,2,0,1:T(8,128)(2,1)}), bf16[1,64,32,128]{3,2,0,1:T(8,128)(2,1)S(1)}, u32[]{:S(2)}, u32[]{:S(2)}) async-start(bf16[1,64,32,128]{3,2,0,1:T(8,128)(2,1)} %fusion.15), calls=%async_computation.1 | async-start | bytes 1048576 | tf_op jit(solution)/shard_map/all_to_all | solution.py:69
  104.9 23.8 %all-to-all-start.2 = ((f32[256,1,192]{2,1,0:T(1,128)}), f32[256,1,192]{2,1,0:T(1,128)S(1)}, u32[]{:S(2)}, u32[]{:S(2)}) async-start(f32[256,1,192]{2,1,0:T(1,128)} %all_to_all.26), calls=%async_computation.2 | async-start | bytes 524288 | tf_op jit(solution)/shard_map/all_to_all | solution.py:83
